TPU v7x, 32 devices: a whole 2x2x4 slice. The times are simulated.
32 devices in a mesh: tok: 8 (over z, y), exp: 4 (over x, core).
Axes of the slice: x: 2, y: 2, z: 4, core: 2. Of those that a mesh axis runs over, the one named last changes fastest.
Arguments:
- tokens: bfloat16 [12, 8192, 1024], P(None, 'tok'), may hold values from -24 to 24
- slot_params: bfloat16 [1024, 128], P(None, 'exp'), may hold values from -2 to 2
- w_in: bfloat16 [64, 1024, 4096], P('exp', None, 'tok'), may hold values from -0.75 to 0.75
- w_out: bfloat16 [64, 4096, 1024], P('exp', 'tok'), may hold values from -0.1875 to 0.1875
Outputs:
- mixed: bfloat16 [12, 8192, 1024], P(None, 'tok', 'exp')
All inputs are finite; a program needn't handle non-finite values.
Results may differ from a plain program's by a relative error of at most 0.0072.
Values may be sent and summed in bfloat16 or wider, within the bound.
A program may use at most 192 MiB of HBM per device.

v0:
```python
import jax
import jax.numpy as jnp
from jax import lax
from jax.sharding import PartitionSpec as P

SLOTS_PER = 2


def shards(tokens, slot_params, w_in, w_out):
    own_width = slot_params.shape[1]
    own_logits = jnp.einsum("std,dj->sjt", tokens, slot_params, preferred_element_type=jnp.float32)
    all_logits = lax.all_gather(own_logits, "exp", axis=1, tiled=True)
    local_max = jnp.max(own_logits, axis=2)
    slot_peak = lax.pmax(local_max, "tok")
    dexp = jnp.exp(own_logits - slot_peak[:, :, None])
    local_den = jnp.sum(dexp, axis=2)
    dweight = dexp.astype(jnp.bfloat16)
    local_sum = jnp.einsum("sjt,std->sjd", dweight, tokens, preferred_element_type=jnp.float32)
    slot_sum, slot_den = lax.psum((local_sum, local_den), "tok")
    slot_in = (slot_sum / slot_den[:, :, None]).astype(jnp.bfloat16)
    seq_count = tokens.shape[0]
    local_experts = w_in.shape[0]
    width = tokens.shape[2]
    grouped = slot_in.reshape(seq_count, local_experts, SLOTS_PER, width)
    hidden = jax.nn.gelu(
        jnp.einsum("sepd,edf->sepf", grouped, w_in, preferred_element_type=jnp.float32),
        approximate=True,
    ).astype(jnp.bfloat16)
    partial_out = jnp.einsum("sepf,efd->sepd", hidden, w_out, preferred_element_type=jnp.float32)
    partial_out = partial_out.reshape(seq_count, own_width, width)
    summed = lax.psum(partial_out, "tok").astype(jnp.bfloat16)
    slot_out = lax.all_to_all(summed, "exp", split_axis=2, concat_axis=1, tiled=True)
    comb_max = jnp.max(all_logits, axis=1)
    cexp = jnp.exp(all_logits - comb_max[:, None, :])
    cweight = (cexp / jnp.sum(cexp, axis=1)[:, None, :]).astype(jnp.bfloat16)
    mixed = jnp.einsum("sjt,sjd->std", cweight, slot_out, preferred_element_type=jnp.float32)
    return mixed.astype(jnp.bfloat16)


def solution(mesh):
    return jax.shard_map(
        shards,
        mesh=mesh,
        in_specs=(
            P(None, "tok", None),
            P(None, "exp"),
            P("exp", None, "tok"),
            P("exp", "tok", None),
        ),
        out_specs=P(None, "tok", "exp"),
        check_vma=False,
    )
```

profile of v0, /device:TPU:0, one launch (start us, length us, event | category | flops | bytes accessed | tf_op | source)
XLA Modules:
  0.0 546.4 jit_solution(2624365932778062341)
XLA Ops:
  7.4 0.0 copy-start
  7.4 0.0 all-reduce.3.cloned.1.call-start
  7.4 0.8 copy-done
  8.2 12.3 %fusion.28 = (f32[12,32]{1,0:T(8,128)S(1)}, f32[12,32,1024]{2,1,0:T(8,128)S(1)}) fusion(bf16[12,1024,1024]{2,1,0:T(8,128)(2,1)} %param.4, bf16[1024,32]{0,1:T(8,128)(2,1)S(1)} %copy-done), kind=kOutput, calls=%fused_computation.28 | convolution fusion | flops 805699200 | bytes 26805760 | tf_op jit(solution)/shard_map/std,dj->sjt/dot_general | solution.py:11
  20.5 0.0 copy-start.2
  20.5 23.4 %pmax.7 = f32[12,32]{1,0:T(8,128)S(1)} all-reduce(f32[12,32]{1,0:T(8,128)S(1)} %get-tuple-element.5), channel_id=1, replica_groups=mesh['tok'=8,'exp'=4] {'tok'}, use_global_device_ids=true, to_apply=%region_3.0 | all-reduce | flops 384 | bytes 3072 | tf_op jit(solution)/shard_map/pmax | solution.py:14
  43.9 11.7 %fusion.23 = f32[12,32,1024]{2,1,0:T(8,128)} fusion(bf16[12,1024,1024]{2,1,0:T(8,128)(2,1)} %param.4, f32[12,32,1024]{2,1,0:T(8,128)S(1)} %get-tuple-element.6, f32[12,32]{1,0:T(8,128)S(1)} %pmax.7), kind=kOutput, calls=%fused_computation.24 | convolution fusion | flops 806092800 | bytes 28313088 | tf_op jit(solution)/shard_map/sjt,std->sjd/dot_general | solution.py:18
  55.6 0.0 copy-done.2
  55.6 0.0 all-reduce.3.cloned.1.call-update
  55.6 0.0 all-gather.2.cloned.1.call-start
  55.6 0.5 all-gather.2.cloned.1.call-update
  56.2 1.8 fusion.6
  57.9 18.4 %psum.22 = f32[12,32]{1,0:T(8,128)S(1)} all-reduce(f32[12,32]{1,0:T(8,128)S(1)} %fusion.6), channel_id=1, replica_groups=mesh['tok'=8,'exp'=4] {'tok'}, use_global_device_ids=true, to_apply=%region_6.0 | all-reduce | flops 384 | bytes 3072 | tf_op jit(solution)/shard_map/psum | solution.py:19
  76.3 66.0 %all-reduce.3.cloned.1.call-done = f32[12,32,1024]{2,1,0:T(8,128)} async-done(((f32[12,32,1024]{2,1,0:T(8,128)}), f32[12,32,1024]{2,1,0:T(8,128)}) %all-reduce.3.cloned.1.call-update) | async-done | bytes 1572880 | tf_op jit(solution)/shard_map/psum | solution.py:19
  142.3 1.6 divide_convert_fusion.2
  144.0 0.4 copy.20
  144.4 8.7 %fusion.20 = bf16[12,16,2,512]{3,0,2,1:T(8,128)(2,1)S(1)} fusion(bf16[12,16,2,1024]{3,0,2,1:T(8,128)(2,1)S(1)} %bitcast.48, bf16[16,1024,512]{2,1,0:T(8,128)(2,1)} %param.6), kind=kOutput, calls=%fused_computation.23 | convolution fusion | flops 404422656 | bytes 17956864 | tf_op jit(solution)/shard_map/sepd,edf->sepf/dot_general | solution.py:26
  153.2 8.7 %fusion.1 = f32[16,12,2,1024]{3,1,2,0:T(8,128)S(1)} fusion(bf16[12,16,2,512]{3,0,2,1:T(8,128)(2,1)S(1)} %fusion.20, bf16[16,512,1024]{2,1,0:T(8,128)(2,1)} %param.7), kind=kOutput, calls=%fused_computation.1 | convolution fusion | flops 402653184 | bytes 18743296 | tf_op jit(solution)/shard_map/sepf,efd->sepd/dot_general | solution.py:29
  161.9 6.5 %copy.13 = f32[12,32,1024]{1,0,2:T(8,128)} copy(f32[12,32,1024]{2,0,1:T(8,128)S(1)} %bitcast.47) | data formatting | bytes 3145728 | tf_op jit(solution)/shard_map/reshape | solution.py:30
  168.4 326.7 %all-reduce.4 = bf16[12,32,1024]{1,0,2:T(8,128)(2,1)} all-reduce(f32[12,32,1024]{1,0,2:T(8,128)} %copy.13), channel_id=1, replica_groups=mesh['tok'=8,'exp'=4] {'tok'}, use_global_device_ids=true, to_apply=%region_7.0 | all-reduce | flops 393216 | bytes 2359296 | tf_op jit(solution)/shard_map/psum | solution.py:31
  495.1 5.0 reshape.15
  500.1 14.2 %all_to_all.18 = bf16[4,2,49152]{2,1,0:T(2,128)(2,1)S(1)} all-to-all(bf16[4,2,49152]{2,1,0:T(2,128)(2,1)S(1)} %reshape.15), channel_id=1, replica_groups=mesh['tok'=8,'exp'=4] {'exp'}, dimensions={0} | all-to-all | bytes 1572864 | tf_op jit(solution)/shard_map/all_to_all | solution.py:32
  514.3 4.1 reshape.16
  518.4 5.1 copy.21
  523.6 0.1 copy.15
  523.7 0.0 all-gather.2.cloned.1.call-done
  523.7 5.8 %fusion.29 = f32[12,1024]{1,0:T(8,128)S(1)} fusion(f32[12,128,1024]{2,1,0:T(8,128)} %all-gather.2.cloned.1.call-done), kind=kOutput, calls=%fused_computation.29 | output fusion | flops 3145855 | bytes 6340608 | tf_op jit(solution)/shard_map/sub | solution.py:34
  529.5 0.0 copy-start.1
  529.6 9.4 %convolution_convert_fusion = bf16[12,1024,256]{2,1,0:T(8,128)(2,1)} fusion(bf16[12,128,256]{2,1,0:T(8,128)(2,1)S(1)} %bitcast.50, f32[12,1024]{1,0:T(8,128)S(1)} %fusion.29, f32[12,128,1024]{2,1,0:T(8,128)} %all-gather.2.cloned.1.call-done), kind=kOutput, calls=%fused_computation.7 | convolution fusion | flops 813183104 | bytes 13418496 | tf_op jit(solution)/shard_map/sjt,sjd->std/dot_general | solution.py:36
  539.0 0.0 copy-done.1
Async XLA Ops:
  7.4 0.8 copy-start
  7.4 135.0 %all-reduce.3.cloned.1.call-start = ((), (), s32[]{:S(2)}) async-start(), calls=%async_computation.2 | async-start | bytes 3145728 | tf_op jit(solution)/shard_map/psum | solution.py:19
  20.5 35.0 %copy-start.2 = (f32[12,32,1024]{2,1,0:T(8,128)}, f32[12,32,1024]{2,1,0:T(8,128)S(1)}, u32[]{:S(2)}) copy-start(f32[12,32,1024]{2,1,0:T(8,128)S(1)} %get-tuple-element.6) | copy-start | bytes 4718596
  55.6 468.1 %all-gather.2.cloned.1.call-start = ((), (), s32[]{:S(2)}) async-start(), calls=%async_computation.1 | async-start | bytes 7864320 | tf_op jit(solution)/shard_map/all_gather | solution.py:12
  529.5 9.4 %copy-start.1 = (bf16[1024,32]{0,1:T(8,128)(2,1)S(1)}, bf16[1024,32]{0,1:T(8,128)(2,1)}, u32[]{:S(2)}) copy-start(bf16[1024,32]{0,1:T(8,128)(2,1)} %param.5) | copy-start | bytes 196612
Sparse Core Ops, SparseCore 0:
  55.7 86.5 all-reduce.2
Sparse Core Ops, SparseCore 1:
  57.6 43.5 all-gather.1
where the time goes:
time: 547 us; the launch traced here: 546 us
  blocking collectives  383 us (70%)
  waiting for transfers between devices  66.6 us (12%)
  matrix products  50.8 us (9%)
  local copies, waits for them, and re-layouts  22.2 us (4%)
  between operations  14.9 us (3%)
  other arithmetic  9.19 us (2%)
    psum x1, blocking collectives, shards(): summed = lax.psum(partial_out, 'tok').astype(jnp.bfloat16)  327 us
    psum x1, waiting for transfers between devices, shards(): slot_sum, slot_den = lax.psum((local_sum, local_den), 'tok')  66 us
    pmax x1, blocking collectives, shards(): slot_peak = lax.pmax(local_max, 'tok')  23.4 us
    psum x1, blocking collectives, shards(): slot_sum, slot_den = lax.psum((local_sum, local_den), 'tok')  18.4 us
    all_to_all x1, blocking collectives, shards(): lax.all_to_all(summed, 'exp', split_axis=2, concat_axis=1, tiled=True)  14.2 us
    dot_general x1, matrix products, shards(): jnp.einsum('std,dj->sjt', tokens, slot_params, preferred_element_type=jnp...  12.3 us
    dot_general x1, matrix products, shards(): jnp.einsum('sjt,std->sjd', dweight, tokens, preferred_element_type=jnp.fl...  11.7 us
  transfers between devices with their start and end apart: 2, of which 1 were waited for; matrix products, arithmetic and copies ran while one was open for 8% of the time, Pallas kernels for 0%

commit v1 on v0

--- a/solution.py
+++ b/solution.py
@@ -29,7 +29,10 @@
     partial_out = jnp.einsum("sepf,efd->sepd", hidden, w_out, preferred_element_type=jnp.float32)
     partial_out = partial_out.reshape(seq_count, own_width, width)
     summed = lax.psum(partial_out, "tok").astype(jnp.bfloat16)
-    slot_out = lax.all_to_all(summed, "exp", split_axis=2, concat_axis=1, tiled=True)
+    size = lax.axis_size("exp")
+    pieces = jnp.stack(jnp.split(summed, size, axis=2), axis=0)
+    pieces = lax.all_to_all(pieces, "exp", split_axis=0, concat_axis=0)
+    slot_out = jnp.concatenate(pieces, axis=1)
     comb_max = jnp.max(all_logits, axis=1)
     cexp = jnp.exp(all_logits - comb_max[:, None, :])
     cweight = (cexp / jnp.sum(cexp, axis=1)[:, None, :]).astype(jnp.bfloat16)

time: 547 us -> 282 us (0.52)
  blocking collectives: 383 us -> 137 us
  local copies, waits for them, and re-layouts: 22.2 us -> 2.36 us
    psum x1, blocking collectives: 327 us -> 81.3 us  [shards(): summed = lax.psum(partial_out, 'tok').astype(jnp.bfloat16)]
    unnamed x8 -> x6, local copies, waits for them, and re-layouts: 9.98 us -> 0.85 us
    reshape x1, local copies, waits for them, and re-layouts: 6.51 us -> 0.92 us  [shards(): partial_out = partial_out.reshape(seq_count, own_width, width)]
where the time goes in v1:
time: 282 us; the launch traced here: 281 us
  blocking collectives  137 us (49%)
  waiting for transfers between devices  66.7 us (24%)
  matrix products  50.9 us (18%)
  between operations  14.9 us (5%)
  other arithmetic  9.29 us (3%)
    psum x1, blocking collectives, shards(): summed = lax.psum(partial_out, 'tok').astype(jnp.bfloat16)  81.3 us
    psum x1, waiting for transfers between devices, shards(): slot_sum, slot_den = lax.psum((local_sum, local_den), 'tok')  66.2 us
    pmax x1, blocking collectives, shards(): slot_peak = lax.pmax(local_max, 'tok')  23.4 us
    psum x1, blocking collectives, shards(): slot_sum, slot_den = lax.psum((local_sum, local_den), 'tok')  18.4 us
    all_to_all x1, blocking collectives, shards(): pieces = lax.all_to_all(pieces, 'exp', split_axis=0, concat_axis=0)  14.1 us
    dot_general x1, matrix products, shards(): jnp.einsum('std,dj->sjt', tokens, slot_params, preferred_element_type=jnp...  12.3 us
    dot_general x1, matrix products, shards(): jnp.einsum('sjt,std->sjd', dweight, tokens, preferred_element_type=jnp.fl...  11.7 us
    dot_general x1, matrix products, shards(): jnp.einsum('sjt,sjd->std', cweight, slot_out, preferred_element_type=jnp....  9.41 us
  transfers between devices with their start and end apart: 2, of which 1 were waited for; matrix products, arithmetic and copies ran while one was open for 8% of the time, Pallas kernels for 0%

profile of v1, /device:TPU:0, one launch (start us, length us, event | category | flops | bytes accessed | tf_op | source)
XLA Modules:
  0.0 281.3 jit_solution(13637341516667016020)
XLA Ops:
  7.4 0.0 copy-start
  7.4 0.0 all-reduce.3.cloned.1.call-start
  7.4 0.8 copy-done
  8.2 12.3 %fusion.28 = (f32[12,32]{1,0:T(8,128)S(1)}, f32[12,32,1024]{2,1,0:T(8,128)S(1)}) fusion(bf16[12,1024,1024]{2,1,0:T(8,128)(2,1)} %param.4, bf16[1024,32]{0,1:T(8,128)(2,1)S(1)} %copy-done), kind=kOutput, calls=%fused_computation.33 | convolution fusion | flops 805699200 | bytes 26805760 | tf_op jit(solution)/shard_map/std,dj->sjt/dot_general | solution.py:11
  20.5 0.0 copy-start.2
  20.5 23.4 %pmax.7 = f32[12,32]{1,0:T(8,128)S(1)} all-reduce(f32[12,32]{1,0:T(8,128)S(1)} %get-tuple-element.9), channel_id=1, replica_groups=mesh['tok'=8,'exp'=4] {'tok'}, use_global_device_ids=true, to_apply=%region_3.0 | all-reduce | flops 384 | bytes 3072 | tf_op jit(solution)/shard_map/pmax | solution.py:14
  43.9 11.7 %fusion.23 = f32[12,32,1024]{2,1,0:T(8,128)} fusion(bf16[12,1024,1024]{2,1,0:T(8,128)(2,1)} %param.4, f32[12,32,1024]{2,1,0:T(8,128)S(1)} %get-tuple-element.10, f32[12,32]{1,0:T(8,128)S(1)} %pmax.7), kind=kOutput, calls=%fused_computation.24 | convolution fusion | flops 806092800 | bytes 28313088 | tf_op jit(solution)/shard_map/sjt,std->sjd/dot_general | solution.py:18
  55.6 0.0 copy-done.2
  55.6 0.0 all-reduce.3.cloned.1.call-update
  55.6 0.0 all-gather.2.cloned.1.call-start
  55.6 0.5 all-gather.2.cloned.1.call-update
  56.2 1.8 fusion.6
  57.9 18.4 %psum.22 = f32[12,32]{1,0:T(8,128)S(1)} all-reduce(f32[12,32]{1,0:T(8,128)S(1)} %fusion.6), channel_id=1, replica_groups=mesh['tok'=8,'exp'=4] {'tok'}, use_global_device_ids=true, to_apply=%region_6.0 | all-reduce | flops 384 | bytes 3072 | tf_op jit(solution)/shard_map/psum | solution.py:19
  76.3 66.2 %all-reduce.3.cloned.1.call-done = f32[12,32,1024]{2,1,0:T(8,128)} async-done(((f32[12,32,1024]{2,1,0:T(8,128)}), f32[12,32,1024]{2,1,0:T(8,128)}) %all-reduce.3.cloned.1.call-update) | async-done | bytes 1572880 | tf_op jit(solution)/shard_map/psum | solution.py:19
  142.5 1.6 divide_convert_fusion.2
  144.1 0.4 copy.15
  144.6 8.7 %fusion.20 = bf16[12,16,2,512]{3,0,2,1:T(8,128)(2,1)S(1)} fusion(bf16[12,16,2,1024]{3,0,2,1:T(8,128)(2,1)S(1)} %bitcast.51, bf16[16,1024,512]{2,1,0:T(8,128)(2,1)} %param.6), kind=kOutput, calls=%fused_computation.23 | convolution fusion | flops 404422656 | bytes 17956864 | tf_op jit(solution)/shard_map/sepd,edf->sepf/dot_general | solution.py:26
  153.3 8.7 %fusion.1 = f32[16,12,2,1024]{3,1,2,0:T(8,128)S(1)} fusion(bf16[12,16,2,512]{3,0,2,1:T(8,128)(2,1)S(1)} %fusion.20, bf16[16,512,1024]{2,1,0:T(8,128)(2,1)} %param.7), kind=kOutput, calls=%fused_computation.1 | convolution fusion | flops 402653184 | bytes 18743296 | tf_op jit(solution)/shard_map/sepf,efd->sepd/dot_general | solution.py:29
  162.0 0.9 copy.9
  163.0 81.3 %all-reduce.4 = bf16[12,32,1024]{2,1,0:T(8,128)(2,1)S(1)} all-reduce(f32[12,32,1024]{2,1,0:T(8,128)S(1)} %copy.9), channel_id=1, replica_groups=mesh['tok'=8,'exp'=4] {'tok'}, use_global_device_ids=true, to_apply=%region_7.0 | all-reduce | flops 393216 | bytes 2359296 | tf_op jit(solution)/shard_map/psum | solution.py:31
  244.3 0.1 slice_bitcast_fusion.3
  244.4 0.1 pad_maximum_fusion
  244.5 14.1 %all_to_all.5 = bf16[4,12,32,256]{3,2,1,0:T(8,128)(2,1)S(1)} all-to-all(bf16[4,12,32,256]{3,2,1,0:T(8,128)(2,1)S(1)} %pad_maximum_fusion), channel_id=1, replica_groups=mesh['tok'=8,'exp'=4] {'exp'}, dimensions={0} | all-to-all | bytes 1572864 | tf_op jit(solution)/shard_map/all_to_all | solution.py:34
  258.6 0.1 copy.10
  258.6 0.0 all-gather.2.cloned.1.call-done
  258.7 5.8 %fusion.29 = f32[12,1024]{1,0:T(8,128)S(1)} fusion(f32[12,128,1024]{2,1,0:T(8,128)} %all-gather.2.cloned.1.call-done), kind=kOutput, calls=%fused_computation.34 | output fusion | flops 3145855 | bytes 6340608 | tf_op jit(solution)/shard_map/sub | solution.py:37
  264.5 0.0 copy-start.1
  264.5 9.4 %convolution_convert_fusion = bf16[12,1024,256]{2,1,0:T(8,128)(2,1)} fusion(bf16[12,128,256]{2,1,0:T(8,128)(2,1)S(1)} %bitcast.53, f32[12,1024]{1,0:T(8,128)S(1)} %fusion.29, f32[12,128,1024]{2,1,0:T(8,128)} %all-gather.2.cloned.1.call-done), kind=kOutput, calls=%fused_computation.7 | convolution fusion | flops 813183104 | bytes 13418496 | tf_op jit(solution)/shard_map/sjt,sjd->std/dot_general | solution.py:39
  273.9 0.0 copy-done.1
Async XLA Ops:
  7.4 0.8 copy-start
  7.4 135.1 %all-reduce.3.cloned.1.call-start = ((), (), s32[]{:S(2)}) async-start(), calls=%async_computation.2 | async-start | bytes 3145728 | tf_op jit(solution)/shard_map/psum | solution.py:19
  20.5 35.0 %copy-start.2 = (f32[12,32,1024]{2,1,0:T(8,128)}, f32[12,32,1024]{2,1,0:T(8,128)S(1)}, u32[]{:S(2)}) copy-start(f32[12,32,1024]{2,1,0:T(8,128)S(1)} %get-tuple-element.10) | copy-start | bytes 4718596
  55.6 203.1 %all-gather.2.cloned.1.call-start = ((), (), s32[]{:S(2)}) async-start(), calls=%async_computation.1 | async-start | bytes 7864320 | tf_op jit(solution)/shard_map/all_gather | solution.py:12
  264.5 9.4 %copy-start.1 = (bf16[1024,32]{0,1:T(8,128)(2,1)S(1)}, bf16[1024,32]{0,1:T(8,128)(2,1)}, u32[]{:S(2)}) copy-start(bf16[1024,32]{0,1:T(8,128)(2,1)} %param.5) | copy-start | bytes 196612
Sparse Core Ops, SparseCore 0:
  55.7 86.7 all-reduce.2
Sparse Core Ops, SparseCore 1:
  57.6 43.5 all-gather.1
